TPU v7x, 32 devices: a whole 2x2x4 slice. The times are simulated.
32 devices in a mesh: dp: 4 (over y, core), space: 4 (over z), tensor: 2 (over x).
Axes of the slice: x: 2, y: 2, z: 4, core: 2. Of those that a mesh axis runs over, the one named last changes fastest.
Arguments:
- feature_map: bfloat16 [4, 32, 48, 1536], P('dp', 'space', None, 'tensor'), may hold values from -12 to 12
- conv_kernel: float32 [7, 7, 1536], replicated, may hold values from -6 to 6
- conv_bias: float32 [1536], replicated, may hold values from -4 to 4
- norm_gain: float32 [1536], replicated, may hold values from 0.1 to 1.9
- norm_bias: float32 [1536], replicated, may hold values from -3 to 3
- expand_weight: bfloat16 [1536, 6144], P(None, 'tensor'), may hold values from -0.21875 to 0.21875
- expand_bias: float32 [6144], P('tensor'), may hold values from -3 to 3
- project_weight: bfloat16 [6144, 1536], P('tensor'), may hold values from -0.109375 to 0.109375
- project_bias: float32 [1536], P('tensor'), may hold values from -3 to 3
- layer_scale: float32 [1536], P('tensor'), may hold values from 0.3 to 1.5
- cotangent: bfloat16 [4, 32, 48, 1536], P('dp', 'space', None, 'tensor'), may hold values from -6 to 6
Outputs:
- block_out: bfloat16 [4, 32, 48, 1536], P('dp', 'space', None, 'tensor')
- grad_input: bfloat16 [4, 32, 48, 1536], P('dp', 'space', None, 'tensor')
- grad_expand: float32 [1536, 6144], P(None, 'tensor')
- grad_project: float32 [6144, 1536], P('tensor')
- grad_kernel: float32 [7, 7, 1536], P(None, None, 'tensor')
All inputs are finite; a program needn't handle non-finite values.
Results may differ from a plain program's by a relative error of at most 0.0067.
Values may be sent and summed in bfloat16 or wider, within the bound.
A program may use at most 192 MiB of HBM per device.

v0:
```python
import jax
import jax.numpy as jnp
from jax import lax
from jax.sharding import PartitionSpec as P

EPSILON = 1e-06
INV_ROOT_TWO = 0.7071067811865476
INV_ROOT_TAU = 0.3989422804014327


def padded_2(block, sides, width):
    for axis, dim in sides:
        count = lax.axis_size(axis)
        forward = [(i, i + 1) for i in range(count - 1)]
        backward = [(target, source) for source, target in forward]
        low = lax.ppermute(
            lax.slice_in_dim(block, block.shape[dim] - width, None, axis=dim), axis, forward
        )
        high = lax.ppermute(lax.slice_in_dim(block, 0, width, axis=dim), axis, backward)
        block = jnp.concatenate([low, block, high], axis=dim)
    return block


def row_rims(block_data):
    return padded_2(block_data, (("space", 1),), 3)


def all_channels(block_data):
    return lax.all_gather(block_data, "tensor", axis=1, tiled=True)


def channel_total(stacked):
    return lax.psum(stacked, "tensor")


def partial_sums(term_rows):
    return lax.psum_scatter(term_rows, "tensor", scatter_dimension=1, tiled=True)


def pixel_total(term, dim):
    shared = lax.psum_scatter(term, ("dp", "space"), scatter_dimension=dim, tiled=True)
    whole = lax.all_gather(shared.astype(jnp.bfloat16), ("dp", "space"), axis=dim, tiled=True)
    return whole.astype(jnp.float32)


def depthwise(padded, tap_weights, row_count, col_count):
    widened = jnp.pad(padded.astype(jnp.float32), ((0, 0), (0, 0), (3, 3), (0, 0)))
    running = jnp.zeros((widened.shape[0], row_count, col_count, widened.shape[3]), jnp.float32)
    for tap_row in range(7):
        for tap_col in range(7):
            running = (
                running
                + tap_weights[tap_row, tap_col]
                * widened[:, tap_row : tap_row + row_count, tap_col : tap_col + col_count, :]
            )
    return running


def kernel_grad(grad_block, padded, row_count, col_count):
    widened = jnp.pad(padded.astype(jnp.float32), ((0, 0), (0, 0), (3, 3), (0, 0)))
    grad_float = grad_block.astype(jnp.float32)
    tap_rows = []
    for tap_row in range(7):
        tap_line = []
        for tap_col in range(7):
            window = widened[:, tap_row : tap_row + row_count, tap_col : tap_col + col_count, :]
            tap_line.append(jnp.sum(grad_float * window, axis=(0, 1, 2)))
        tap_rows.append(jnp.stack(tap_line))
    return jnp.stack(tap_rows)


def gelu_slope(values):
    cumulative = 0.5 * (1.0 + lax.erf(values * INV_ROOT_TWO))
    density = jnp.exp(-0.5 * values * values) * INV_ROOT_TAU
    return cumulative + values * density


def body(
    feature_map,
    conv_kernel,
    conv_bias,
    norm_gain,
    norm_bias,
    expand_weight,
    expand_bias,
    project_weight,
    project_bias,
    layer_scale,
    cotangent,
):
    images, row_count, col_count, shard_width = feature_map.shape
    pixels = images * row_count * col_count
    full_width = expand_weight.shape[0]
    offset = lax.axis_index("tensor") * shard_width
    own_gain = lax.dynamic_slice_in_dim(norm_gain, offset, shard_width, 0)
    own_kernel = lax.dynamic_slice_in_dim(conv_kernel, offset, shard_width, 2)
    padded = row_rims(feature_map)
    own_bias = lax.dynamic_slice_in_dim(conv_bias, offset, shard_width, 0)
    own_shift = lax.dynamic_slice_in_dim(norm_bias, offset, shard_width, 0)
    filtered = (depthwise(padded, own_kernel, row_count, col_count) + own_bias).reshape(
        pixels, shard_width
    )
    average = channel_total(jnp.sum(filtered, axis=1)) / full_width
    centered = filtered - average[:, None]
    spread = channel_total(jnp.sum(centered * centered, axis=1)) / full_width
    inverse = lax.rsqrt(spread + EPSILON)[:, None]
    unit_norm = centered * inverse
    gathered = all_channels((unit_norm * own_gain + own_shift).astype(jnp.bfloat16))
    hidden = jnp.dot(gathered, expand_weight, preferred_element_type=jnp.float32) + expand_bias
    activated = jax.nn.gelu(hidden, approximate=False).astype(jnp.bfloat16)
    projected = partial_sums(jnp.dot(activated, project_weight, preferred_element_type=jnp.float32))
    residual = feature_map.reshape(pixels, shard_width).astype(jnp.float32)
    block_out = (
        (residual + layer_scale * (projected + project_bias))
        .astype(jnp.bfloat16)
        .reshape(feature_map.shape)
    )
    grad_scaled = (cotangent.reshape(pixels, shard_width).astype(jnp.float32) * layer_scale).astype(
        jnp.bfloat16
    )
    grad_full = all_channels(grad_scaled)
    grad_project = pixel_total(
        lax.dot_general(
            activated, grad_full, (((0,), (0,)), ((), ())), preferred_element_type=jnp.float32
        ),
        1,
    )
    grad_act = lax.dot_general(
        grad_full, project_weight, (((1,), (1,)), ((), ())), preferred_element_type=jnp.float32
    )
    grad_hidden = (grad_act * gelu_slope(hidden)).astype(jnp.bfloat16)
    grad_expand = pixel_total(
        lax.dot_general(
            gathered, grad_hidden, (((0,), (0,)), ((), ())), preferred_element_type=jnp.float32
        ),
        0,
    )
    normed_terms = lax.dot_general(
        grad_hidden, expand_weight, (((1,), (1,)), ((), ())), preferred_element_type=jnp.float32
    )
    grad_normed = partial_sums(normed_terms)
    scaled_grad = grad_normed * own_gain
    channel_means = (
        lax.psum(
            jnp.stack([jnp.sum(scaled_grad, axis=1), jnp.sum(scaled_grad * unit_norm, axis=1)]),
            "tensor",
        )
        / full_width
    )
    grad_filtered = (
        (scaled_grad - channel_means[0][:, None] - unit_norm * channel_means[1][:, None]) * inverse
    ).astype(jnp.bfloat16)
    grad_block = grad_filtered.reshape(images, row_count, col_count, shard_width)
    grad_kernel = kernel_grad(grad_block, padded, row_count, col_count)
    grad_padded = row_rims(grad_block)
    grad_input = (
        cotangent.astype(jnp.float32)
        + depthwise(grad_padded, own_kernel[::-1, ::-1], row_count, col_count)
    ).astype(jnp.bfloat16)
    grad_kernel = lax.psum(grad_kernel, ("dp", "space"))
    return (block_out, grad_input, grad_expand, grad_project, grad_kernel)


def solution(mesh):
    in_specs = (
        P("dp", "space", None, "tensor"),
        P(),
        P(),
        P(),
        P(),
        P(None, "tensor"),
        P("tensor"),
        P("tensor", None),
        P("tensor"),
        P("tensor"),
        P("dp", "space", None, "tensor"),
    )
    out_specs = (
        P("dp", "space", None, "tensor"),
        P("dp", "space", None, "tensor"),
        P(None, "tensor"),
        P("tensor", None),
        P(None, None, "tensor"),
    )
    return jax.shard_map(body, mesh=mesh, in_specs=in_specs, out_specs=out_specs, check_vma=False)
```

profile of v0, /device:TPU:1, one launch (start us, length us, event | category | flops | bytes accessed | tf_op | source)
XLA Modules:
  0.0 874.0 jit_solution(9765757772026388206)
XLA Ops:
  7.2 0.0 all-gather.5.cloned.1.call-start
  7.2 1.1 fusion.175
  8.4 4.0 collective-permute-start
  12.4 1.3 collective-permute-start.1
  13.7 0.8 dynamic_slice.14
  14.5 0.8 dynamic_slice.13
  15.2 0.8 dynamic_slice.15
  16.0 2.4 fusion.161
  18.5 1.8 collective-permute-done.1
  20.3 0.2 maximum_convert_fusion
  20.5 12.7 %fusion.173 = (f32[8,48]{1,0:T(8,128)S(1)}, f32[1,8,48,768]{3,2,1,0:T(8,128)S(1)}) fusion(f32[768]{0:T(1024)S(1)} %dynamic_slice.13, f32[768]{0:T(1024)S(1)} %get-tuple-element.109, f32[768]{0:T(1024)S(1)} %get-tuple-element.62, f32[768]{0:T(1024)S(1)} %get-tuple-element.63, f32[1,14,48,768]{3,2,1,0:T(8,128)S(1)} %maximum_convert_fusion, ...), kind=kLoop, calls=%fused_computation.396 | loop fusion | flops 29195904 | bytes 11707904 | tf_op jit(solution)/shard_map/reduce_sum | solution.py:103
  33.2 0.1 reduce_sum.482
  33.3 3.8 psum.28
  37.1 0.1 sub.30
  37.1 0.3 multiply_reduce_fusion.1
  37.4 0.1 reduce_sum.484
  37.5 3.8 psum.29
  41.3 1.1 add_convert_fusion
  42.3 0.0 all-gather.5.cloned.1.call-update
  42.4 0.0 reduce-scatter.5.cloned.1.call-start
  42.4 26.4 %all-gather.5.cloned.1.call-done = bf16[384,1536]{1,0:T(8,128)(2,1)} async-done(((bf16[384,768]{1,0:T(8,128)(2,1)}), bf16[384,1536]{1,0:T(8,128)(2,1)}) %all-gather.5.cloned.1.call-update) | async-done | bytes 1179664 | tf_op jit(solution)/shard_map/all_gather | solution.py:29
  68.8 17.0 %fusion.2 = (bf16[384,3072]{1,0:T(8,128)(2,1)S(1)}, f32[384,3072]{1,0:T(8,128)}) fusion(f32[3072]{0:T(1024)S(1)} %copy-done.10, bf16[384,1536]{1,0:T(8,128)(2,1)} %all-gather.5.cloned.1.call-done, bf16[1536,3072]{1,0:T(8,128)(2,1)} %param.16), kind=kOutput, calls=%fused_computation.53 | convolution fusion | flops 3701735424 | bytes 17707008 | tf_op jit(solution)/shard_map/dot_general | solution.py:109
  85.8 1.4 copy-done.3
  87.1 7.7 fusion.176
  94.9 0.0 reduce-scatter.5.cloned.1.call-update
  94.9 0.0 all-gather.7.cloned.1.call-start
  95.0 34.9 %reduce-scatter.5.cloned.1.call-done = f32[384,768]{1,0:T(8,128)} async-done(((f32[384,1536]{1,0:T(8,128)}), f32[384,768]{1,0:T(8,128)}) %reduce-scatter.5.cloned.1.call-update) | async-done | bytes 1179664 | tf_op jit(solution)/shard_map/reduce_scatter | solution.py:37
  129.8 2.9 fusion.158
  132.7 0.2 reduce-scatter.9.cloned.1.call-start
  133.0 22.7 %all-gather.7.cloned.1.call-done = bf16[384,1536]{1,0:T(8,128)(2,1)} async-done(((bf16[384,768]{1,0:T(8,128)(2,1)}), bf16[384,1536]{1,0:T(8,128)(2,1)}) %all-gather.7.cloned.1.call-update) | async-done | bytes 1179664 | tf_op jit(solution)/shard_map/all_gather | solution.py:29
  155.7 8.4 fusion.8
  164.0 1.4 copy-done.4
  165.5 9.5 %fusion.178 = f32[1536,3072]{1,0:T(8,128)} fusion(bf16[384,1536]{1,0:T(8,128)(2,1)S(1)} %copy-done.6, bf16[384,3072]{1,0:T(8,128)(2,1)S(1)} %fusion.8), kind=kOutput, calls=%fused_computation.401 | convolution fusion | flops 3623878656 | bytes 22413312 | tf_op jit(solution)/shard_map/dot_general | solution.py:133
  175.0 0.0 reduce-scatter.11.cloned.1.call-start
  175.0 13.7 %fusion.179 = f32[3072,1536]{0,1:T(8,128)} fusion(bf16[384,3072]{1,0:T(8,128)(2,1)} %copy-done.3, bf16[384,1536]{1,0:T(8,128)(2,1)} %all-gather.7.cloned.1.call-done), kind=kOutput, calls=%fused_computation.402 | convolution fusion | flops 3623878656 | bytes 22413312 | tf_op jit(solution)/shard_map/dot_general | solution.py:123
  188.8 0.0 reduce-scatter.7.cloned.1.call-start
  188.8 12.0 %fusion.177 = f32[384,1536]{1,0:T(8,128)} fusion(bf16[384,3072]{1,0:T(8,128)(2,1)} %copy-done.4, bf16[1536,3072]{1,0:T(8,128)(2,1)} %param.16), kind=kOutput, calls=%fused_computation.400 | convolution fusion | flops 3623878656 | bytes 14155776 | tf_op jit(solution)/shard_map/dot_general | solution.py:138
  200.8 0.0 all-gather.9.cloned.1.call-start
  200.9 168.3 %reduce-scatter.9.cloned.1.call-done = f32[96,3072]{1,0:T(8,128)} async-done(((f32[1536,3072]{1,0:T(8,128)}), f32[96,3072]{1,0:T(8,128)}) %reduce-scatter.9.cloned.1.call-update) | async-done | bytes 1179664 | tf_op jit(solution)/shard_map/reduce_scatter | solution.py:41
  369.2 2.2 convert_element_type.100
  371.4 0.0 all-gather.11.cloned.1.call-start
  371.4 195.5 %reduce-scatter.11.cloned.1.call-done = f32[3072,96]{0,1:T(8,128)} async-done(((f32[3072,1536]{0,1:T(8,128)}), f32[3072,96]{0,1:T(8,128)}) %reduce-scatter.11.cloned.1.call-update) | async-done | bytes 1179664 | tf_op jit(solution)/shard_map/reduce_scatter | solution.py:41
  566.9 2.2 convert_element_type.102
  569.1 0.0 all-reduce.4.cloned.1.call-start
  569.2 33.8 %reduce-scatter.7.cloned.1.call-done = f32[384,768]{1,0:T(8,128)} async-done(((f32[384,1536]{1,0:T(8,128)}), f32[384,768]{1,0:T(8,128)}) %reduce-scatter.7.cloned.1.call-update) | async-done | bytes 1179664 | tf_op jit(solution)/shard_map/reduce_scatter | solution.py:37
  602.9 1.7 multiply_reduce_fusion.2
  604.6 4.0 psum.30
  608.6 1.6 multiply_convert_fusion
  610.3 2.0 fusion.153
  612.5 2.9 fusion.154
  615.4 2.9 fusion.155
  618.8 3.2 collective-permute-start.2
  622.1 1.3 collective-permute-start.3
  623.8 0.7 copy-done.7
  624.5 6.9 collective-permute-done.2
  631.4 9.2 %collective-permute-done.3 = bf16[1,3,48,768]{3,2,1,0:T(8,128)(2,1)S(1)} collective-permute-done((bf16[1,3,48,768]{3,2,1,0:T(8,128)(2,1)S(1)}, bf16[1,3,48,768]{3,2,1,0:T(8,128)(2,1)S(1)}, u32[]{:S(2)}, u32[]{:S(2)}) %collective-permute-start.3) | collective-permute-done | bytes 221216 | tf_op jit(solution)/shard_map/ppermute | solution.py:19
  640.6 0.2 maximum_convert_fusion.1
  640.7 9.7 %fusion.104 = bf16[1,8,48,768]{3,2,1,0:T(8,128)(2,1)} fusion(f32[1,14,48,768]{3,2,1,0:T(8,128)S(1)} %maximum_convert_fusion.1, f32[768]{0:T(1024)S(1)} %get-tuple-element.109, f32[768]{0:T(1024)S(1)} %get-tuple-element.62, f32[768]{0:T(1024)S(1)} %get-tuple-element.63, f32[768]{0:T(1024)S(1)} %get-tuple-element.64, f32[768]{0:T(1024)S(1)} %get-tuple-element.65, ...), kind=kLoop, calls=%fused_computation.247 | loop fusion | flops 29491200 | bytes 11702272 | tf_op jit(solution)/shard_map/convert_element_type | solution.py:159
  650.4 41.7 %all-gather.9.cloned.1.call-done = bf16[1536,3072]{1,0:T(8,128)(2,1)} async-done(((bf16[96,3072]{1,0:T(8,128)(2,1)}), bf16[1536,3072]{1,0:T(8,128)(2,1)}) %all-gather.9.cloned.1.call-update) | async-done | bytes 9437200 | tf_op jit(solution)/shard_map/all_gather | solution.py:42
  692.1 12.7 %convert_element_type.101 = f32[1536,3072]{1,0:T(8,128)} convert(bf16[1536,3072]{1,0:T(8,128)(2,1)} %all-gather.9.cloned.1.call-done) | non-fusion elementwise | flops 4718592 | bytes 28311552 | tf_op jit(solution)/shard_map/convert_element_type | solution.py:43
  704.8 68.9 %all-gather.11.cloned.1.call-done = bf16[3072,1536]{0,1:T(8,128)(2,1)} async-done(((bf16[3072,96]{0,1:T(8,128)(2,1)}), bf16[3072,1536]{0,1:T(8,128)(2,1)}) %all-gather.11.cloned.1.call-update) | async-done | bytes 9437200 | tf_op jit(solution)/shard_map/all_gather | solution.py:42
  773.7 13.5 %copy.16 = f32[3072,1536]{1,0:T(8,128)} copy(bf16[3072,1536]{0,1:T(8,128)(2,1)} %all-gather.11.cloned.1.call-done) | data formatting | bytes 28311552
  787.3 78.6 %all-reduce.4.cloned.1.call-done = f32[7,7,768]{2,1,0:T(8,128)} async-done(((f32[7,7,768]{2,1,0:T(8,128)}), f32[7,7,768]{2,1,0:T(8,128)}) %all-reduce.4.cloned.1.call-update) | async-done | bytes 150544 | tf_op jit(solution)/shard_map/psum | solution.py:160
  865.9 1.6 copy.24
  (98 shorter events, 0.8 us)
Async XLA Ops:
  7.2 13.2 %copy-start.2 = (bf16[1,8,48,768]{3,2,1,0:T(8,128)(2,1)S(1)}, bf16[1,8,48,768]{3,2,1,0:T(8,128)(2,1)}, u32[]{:S(2)}) copy-start(bf16[1,8,48,768]{3,2,1,0:T(8,128)(2,1)} %param.11) | copy-start | bytes 1769476
  7.2 61.6 %all-gather.5.cloned.1.call-start = ((), (), s32[]{:S(2)}) async-start(), calls=%async_computation.4 | async-start | bytes 1769472 | tf_op jit(solution)/shard_map/all_gather | solution.py:29
  8.4 10.1 %collective-permute-start = (bf16[1,3,48,768]{3,2,1,0:T(8,128)(2,1)S(1)}, bf16[1,3,48,768]{3,2,1,0:T(8,128)(2,1)S(1)}, u32[]{:S(2)}, u32[]{:S(2)}) collective-permute-start(bf16[1,3,48,768]{3,2,1,0:T(8,128)(2,1)S(1)} %get-tuple-element.116), channel_id=1, source_target_pairs={{0,2},{2,4},{4,6},{1,3},{3,5},{5,7},{8,10},{10,12},{12,14},{9,11},... | collective-permute-start | bytes 663560 | tf_op jit(solution)/shard_map/ppermute | solution.py:16
  12.4 7.9 collective-permute-start.1
  41.3 27.5 %copy-start.10 = (f32[3072]{0:T(1024)S(1)}, f32[3072]{0:T(1024)}, u32[]{:S(2)}) copy-start(f32[3072]{0:T(1024)} %param.17) | copy-start | bytes 36868
  42.4 87.5 %reduce-scatter.5.cloned.1.call-start = ((), (), s32[]{:S(2)}) async-start(), calls=%async_computation.5 | async-start | bytes 3538944 | tf_op jit(solution)/shard_map/reduce_scatter | solution.py:37
  85.7 1.4 copy-start.3
  94.9 35.0 %copy-start.8 = (f32[768]{0:T(1024)S(1)}, f32[768]{0:T(1024)}, u32[]{:S(2)}) copy-start(f32[768]{0:T(1024)} %param.20) | copy-start | bytes 9220
  94.9 35.0 %copy-start.9 = (f32[768]{0:T(1024)S(1)}, f32[768]{0:T(1024)}, u32[]{:S(2)}) copy-start(f32[768]{0:T(1024)} %param.19) | copy-start | bytes 9220
  94.9 60.7 %all-gather.7.cloned.1.call-start = ((), (), s32[]{:S(2)}) async-start(), calls=%async_computation.6 | async-start | bytes 1769472 | tf_op jit(solution)/shard_map/all_gather | solution.py:29
  132.7 236.5 %reduce-scatter.9.cloned.1.call-start = ((), (), s32[]{:S(2)}) async-start(), calls=%async_computation.8 | async-start | bytes 20054016 | tf_op jit(solution)/shard_map/reduce_scatter | solution.py:41
  155.7 9.8 %copy-start.6 = (bf16[384,1536]{1,0:T(8,128)(2,1)S(1)}, bf16[384,1536]{1,0:T(8,128)(2,1)}, u32[]{:S(2)}) copy-start(bf16[384,1536]{1,0:T(8,128)(2,1)} %all-gather.5.cloned.1.call-done) | copy-start | bytes 3538948
  164.0 1.4 copy-start.4
  175.0 391.9 %reduce-scatter.11.cloned.1.call-start = ((), (), s32[]{:S(2)}) async-start(), calls=%async_computation.10 | async-start | bytes 20054016 | tf_op jit(solution)/shard_map/reduce_scatter | solution.py:41
  188.8 414.1 %reduce-scatter.7.cloned.1.call-start = ((), (), s32[]{:S(2)}) async-start(), calls=%async_computation.7 | async-start | bytes 3538944 | tf_op jit(solution)/shard_map/reduce_scatter | solution.py:37
  200.8 491.3 %all-gather.9.cloned.1.call-start = ((), (), s32[]{:S(2)}) async-start(), calls=%async_computation.9 | async-start | bytes 10027008 | tf_op jit(solution)/shard_map/all_gather | solution.py:42
  371.4 402.3 %all-gather.11.cloned.1.call-start = ((), (), s32[]{:S(2)}) async-start(), calls=%async_computation.11 | async-start | bytes 10027008 | tf_op jit(solution)/shard_map/all_gather | solution.py:42
  569.1 296.8 %all-reduce.4.cloned.1.call-start = ((), (), s32[]{:S(2)}) async-start(), calls=%async_computation.12 | async-start | bytes 344064 | tf_op jit(solution)/shard_map/psum | solution.py:160
  610.3 8.5 copy-start
  618.8 21.8 %copy-start.1 = (bf16[384,768]{1,0:T(8,128)(2,1)S(1)}, bf16[384,768]{1,0:T(8,128)(2,1)}, u32[]{:S(2)}) copy-start(bf16[384,768]{1,0:T(8,128)(2,1)} %copy-done) | copy-start | bytes 1769476
  618.8 12.5 %collective-permute-start.2 = (bf16[1,3,48,768]{3,2,1,0:T(8,128)(2,1)S(1)}, bf16[1,3,48,768]{3,2,1,0:T(8,128)(2,1)S(1)}, u32[]{:S(2)}, u32[]{:S(2)}) collective-permute-start(bf16[1,3,48,768]{3,2,1,0:T(8,128)(2,1)S(1)} %get-tuple-element.114), channel_id=1, source_target_pairs={{0,2},{2,4},{4,6},{1,3},{3,5},{5,7},{8,10},{10,12},{12,14},{9,11},... | collective-permute-start | bytes 663560 | tf_op jit(solution)/shard_map/ppermute | solution.py:16
  622.1 18.5 %collective-permute-start.3 = (bf16[1,3,48,768]{3,2,1,0:T(8,128)(2,1)S(1)}, bf16[1,3,48,768]{3,2,1,0:T(8,128)(2,1)S(1)}, u32[]{:S(2)}, u32[]{:S(2)}) collective-permute-start(bf16[1,3,48,768]{3,2,1,0:T(8,128)(2,1)S(1)} %get-tuple-element.115), channel_id=1, source_target_pairs={{2,0},{4,2},{6,4},{3,1},{5,3},{7,5},{10,8},{12,10},{14,12},{11,9},... | collective-permute-start | bytes 663560 | tf_op jit(solution)/shard_map/ppermute | solution.py:19
  623.8 0.7 copy-start.7
  624.5 16.2 %copy-start.5 = (bf16[1,8,48,768]{3,2,1,0:T(8,128)(2,1)S(1)}, bf16[1,8,48,768]{3,2,1,0:T(8,128)(2,1)}, u32[]{:S(2)}) copy-start(bf16[1,8,48,768]{3,2,1,0:T(8,128)(2,1)} %param.21) | copy-start | bytes 1769476
Sparse Core Ops, SparseCore 0:
  42.5 26.2 all-gather.4
  95.0 34.7 reduce-scatter.4
  132.9 22.7 all-gather.6
  175.1 194.0 reduce-scatter.8
  373.7 193.1 reduce-scatter.10
  569.0 33.8 reduce-scatter.6
  605.8 86.2 all-gather.8
  694.4 79.2 all-gather.10
  777.7 88.1 all-reduce.3
where the time goes:
time: 875 us; the launch traced here: 874 us
  waiting for transfers between devices  689 us (79%)
  matrix products  68.3 us (8%)
  other arithmetic  55.1 us (6%)
  local copies, waits for them, and re-layouts  25.4 us (3%)
  between operations  14.5 us (2%)
  blocking collectives  11.5 us (1%)
  starting transfers between devices  10.4 us (1%)
    reduce_scatter x2, waiting for transfers between devices, pixel_total(): lax.psum_scatter(term, ('dp', 'space'), scatter_dimension=dim, tiled=True)  364 us
    all_gather x2, waiting for transfers between devices, pixel_total(): lax.all_gather(shared.astype(jnp.bfloat16), ('dp', 'space'), axis=dim, ti...  111 us
    psum x1, waiting for transfers between devices, body(): grad_kernel = lax.psum(grad_kernel, ('dp', 'space'))  78.6 us
    reduce_scatter x2, waiting for transfers between devices, partial_sums(): lax.psum_scatter(term_rows, 'tensor', scatter_dimension=1, tiled=True)  68.6 us
    all_gather x2, waiting for transfers between devices, all_channels(): return lax.all_gather(block_data, 'tensor', axis=1, tiled=True)  49.1 us
    unnamed x30, local copies, waits for them, and re-layouts  18.7 us
  transfers between devices with their start and end apart: 13, of which 12 were waited for; matrix products, arithmetic and copies ran while one was open for 9% of the time, Pallas kernels for 0%

commit v1 on v0

--- a/solution.py
+++ b/solution.py
@@ -157,7 +157,7 @@
         cotangent.astype(jnp.float32)
         + depthwise(grad_padded, own_kernel[::-1, ::-1], row_count, col_count)
     ).astype(jnp.bfloat16)
-    grad_kernel = lax.psum(grad_kernel, ("dp", "space"))
+    grad_kernel = lax.all_gather(grad_kernel, axis_name=("dp", "space")).sum(axis=0)
     return (block_out, grad_input, grad_expand, grad_project, grad_kernel)
 
 

time: 875 us -> 836 us (0.955)
  waiting for transfers between devices: 689 us -> 655 us
    psum x1 -> x0, waiting for transfers between devices: 78.6 us -> none  [body(): grad_kernel = lax.psum(grad_kernel, ('dp', 'space'))]
    all_gather x2, waiting for transfers between devices: 111 us -> 149 us  [pixel_total(): lax.all_gather(shared.astype(jnp.bfloat16), ('dp', 'space'), axis=dim, ti...]
    all_gather x0 -> x1, waiting for transfers between devices: none -> 23.9 us  [body(): lax.all_gather(grad_kernel, axis_name=('dp', 'space')).sum(axis=0)]
    reduce_scatter x2, waiting for transfers between devices: 68.6 us -> 47.1 us  [partial_sums(): lax.psum_scatter(term_rows, 'tensor', scatter_dimension=1, tiled=True)]
    reduce_scatter x2, waiting for transfers between devices: 364 us -> 377 us  [pixel_total(): lax.psum_scatter(term, ('dp', 'space'), scatter_dimension=dim, tiled=True)]
    unnamed x30 -> x27, local copies, waits for them, and re-layouts: 18.7 us -> 17.1 us
  transfers between devices with their start and end apart: 13 -> 13, of which waited for: 12 -> 12; matrix products, arithmetic and copies ran while one was open for 9% -> 8% of each run, Pallas kernels for 0% -> 0%
where the time goes in v1:
time: 836 us; the launch traced here: 835 us
  waiting for transfers between devices  655 us (78%)
  matrix products  63.3 us (8%)
  other arithmetic  57.8 us (7%)
  local copies, waits for them, and re-layouts  23.8 us (3%)
  between operations  14.5 us (2%)
  blocking collectives  11.5 us (1%)
  starting transfers between devices  9.08 us (1%)
    reduce_scatter x2, waiting for transfers between devices, pixel_total(): lax.psum_scatter(term, ('dp', 'space'), scatter_dimension=dim, tiled=True)  377 us
    all_gather x2, waiting for transfers between devices, pixel_total(): lax.all_gather(shared.astype(jnp.bfloat16), ('dp', 'space'), axis=dim, ti...  149 us
    all_gather x2, waiting for transfers between devices, all_channels(): return lax.all_gather(block_data, 'tensor', axis=1, tiled=True)  49.1 us
    reduce_scatter x2, waiting for transfers between devices, partial_sums(): lax.psum_scatter(term_rows, 'tensor', scatter_dimension=1, tiled=True)  47.1 us
    all_gather x1, waiting for transfers between devices, body(): lax.all_gather(grad_kernel, axis_name=('dp', 'space')).sum(axis=0)  23.9 us
    unnamed x27, local copies, waits for them, and re-layouts  17.1 us
    dot_general x1, matrix products, body(): jnp.dot(gathered, expand_weight, preferred_element_type=jnp.float32)  17 us
  transfers between devices with their start and end apart: 13, of which 12 were waited for; matrix products, arithmetic and copies ran while one was open for 8% of the time, Pallas kernels for 0%

profile of v1, /device:TPU:1, one launch (start us, length us, event | category | flops | bytes accessed | tf_op | source)
XLA Modules:
  0.0 835.0 jit_solution(14128379969573443042)
XLA Ops:
  7.2 0.0 all-gather.7.cloned.1.call-start
  7.2 1.1 fusion.175
  8.4 4.0 collective-permute-start
  12.4 1.3 collective-permute-start.1
  13.7 0.8 dynamic_slice.14
  14.5 0.8 dynamic_slice.13
  15.2 0.8 dynamic_slice.15
  16.0 2.4 fusion.161
  18.5 1.8 collective-permute-done.1
  20.3 0.2 maximum_convert_fusion
  20.5 12.7 %fusion.173 = (f32[8,48]{1,0:T(8,128)S(1)}, f32[1,8,48,768]{3,2,1,0:T(8,128)S(1)}) fusion(f32[768]{0:T(1024)S(1)} %dynamic_slice.13, f32[768]{0:T(1024)S(1)} %get-tuple-element.114, f32[768]{0:T(1024)S(1)} %get-tuple-element.67, f32[768]{0:T(1024)S(1)} %get-tuple-element.68, f32[1,14,48,768]{3,2,1,0:T(8,128)S(1)} %maximum_convert_fusion, ...), kind=kLoop, calls=%fused_computation.396 | loop fusion | flops 29195904 | bytes 11707904 | tf_op jit(solution)/shard_map/reduce_sum | solution.py:103
  33.2 0.1 reduce_sum.491
  33.3 3.8 psum.21
  37.1 0.1 sub.30
  37.1 0.3 multiply_reduce_fusion.1
  37.4 0.1 reduce_sum.493
  37.5 3.8 psum.22
  41.3 1.1 add_convert_fusion
  42.3 0.0 all-gather.7.cloned.1.call-update
  42.4 0.0 reduce-scatter.5.cloned.1.call-start
  42.4 26.4 %all-gather.7.cloned.1.call-done = bf16[384,1536]{1,0:T(8,128)(2,1)} async-done(((bf16[384,768]{1,0:T(8,128)(2,1)}), bf16[384,1536]{1,0:T(8,128)(2,1)}) %all-gather.7.cloned.1.call-update) | async-done | bytes 1179664 | tf_op jit(solution)/shard_map/all_gather | solution.py:29
  68.8 17.0 %fusion.2 = (bf16[384,3072]{1,0:T(8,128)(2,1)S(1)}, f32[384,3072]{1,0:T(8,128)}) fusion(f32[3072]{0:T(1024)S(1)} %copy-done.9, bf16[384,1536]{1,0:T(8,128)(2,1)} %all-gather.7.cloned.1.call-done, bf16[1536,3072]{1,0:T(8,128)(2,1)} %param.16), kind=kOutput, calls=%fused_computation.53 | convolution fusion | flops 3701735424 | bytes 17707008 | tf_op jit(solution)/shard_map/dot_general | solution.py:109
  85.8 1.4 copy-done.3
  87.2 7.7 fusion.176
  94.9 0.0 reduce-scatter.5.cloned.1.call-update
  94.9 0.0 all-gather.9.cloned.1.call-start
  95.0 34.9 %reduce-scatter.5.cloned.1.call-done = f32[384,768]{1,0:T(8,128)} async-done(((f32[384,1536]{1,0:T(8,128)}), f32[384,768]{1,0:T(8,128)}) %reduce-scatter.5.cloned.1.call-update) | async-done | bytes 1179664 | tf_op jit(solution)/shard_map/reduce_scatter | solution.py:37
  129.9 2.9 fusion.158
  132.8 0.2 reduce-scatter.7.cloned.1.call-start
  133.0 22.7 %all-gather.9.cloned.1.call-done = bf16[384,1536]{1,0:T(8,128)(2,1)} async-done(((bf16[384,768]{1,0:T(8,128)(2,1)}), bf16[384,1536]{1,0:T(8,128)(2,1)}) %all-gather.9.cloned.1.call-update) | async-done | bytes 1179664 | tf_op jit(solution)/shard_map/all_gather | solution.py:29
  155.7 8.3 fusion.8
  164.0 1.4 copy-done.4
  165.4 7.8 fusion.177
  173.2 0.0 reduce-scatter.9.cloned.1.call-start
  173.3 11.1 %fusion.178 = f32[1536,3072]{1,0:T(8,128)} fusion(bf16[384,1536]{1,0:T(8,128)(2,1)} %all-gather.7.cloned.1.call-done, bf16[384,3072]{1,0:T(8,128)(2,1)} %copy-done.4), kind=kOutput, calls=%fused_computation.401 | convolution fusion | flops 3623878656 | bytes 22413312 | tf_op jit(solution)/shard_map/dot_general | solution.py:133
  184.4 0.0 reduce-scatter.11.cloned.1.call-start
  184.5 11.4 %fusion.179 = f32[3072,1536]{0,1:T(8,128)} fusion(bf16[384,3072]{1,0:T(8,128)(2,1)} %copy-done.3, bf16[384,1536]{1,0:T(8,128)(2,1)} %all-gather.9.cloned.1.call-done), kind=kOutput, calls=%fused_computation.402 | convolution fusion | flops 3623878656 | bytes 22413312 | tf_op jit(solution)/shard_map/dot_general | solution.py:123
  195.9 0.0 all-gather.15.cloned.1.call-start
  195.9 12.2 %reduce-scatter.7.cloned.1.call-done = f32[384,768]{1,0:T(8,128)} async-done(((f32[384,1536]{1,0:T(8,128)}), f32[384,768]{1,0:T(8,128)}) %reduce-scatter.7.cloned.1.call-update) | async-done | bytes 1179664 | tf_op jit(solution)/shard_map/reduce_scatter | solution.py:37
  208.1 1.7 multiply_reduce_fusion.2
  209.8 4.0 psum.23
  213.9 1.6 multiply_convert_fusion
  215.5 2.0 fusion.153
  217.7 2.9 fusion.154
  220.6 2.9 fusion.155
  224.4 0.7 copy-done.6
  225.1 0.0 all-gather.11.cloned.1.call-start
  225.2 181.7 %reduce-scatter.9.cloned.1.call-done = f32[96,3072]{1,0:T(8,128)} async-done(((f32[1536,3072]{1,0:T(8,128)}), f32[96,3072]{1,0:T(8,128)}) %reduce-scatter.9.cloned.1.call-update) | async-done | bytes 1179664 | tf_op jit(solution)/shard_map/reduce_scatter | solution.py:41
  406.8 2.2 convert_element_type.100
  409.0 0.0 all-gather.13.cloned.1.call-start
  409.1 195.5 %reduce-scatter.11.cloned.1.call-done = f32[3072,96]{0,1:T(8,128)} async-done(((f32[3072,1536]{0,1:T(8,128)}), f32[3072,96]{0,1:T(8,128)}) %reduce-scatter.11.cloned.1.call-update) | async-done | bytes 1179664 | tf_op jit(solution)/shard_map/reduce_scatter | solution.py:41
  604.6 2.2 convert_element_type.102
  606.8 1.8 collective-permute-start.2
  608.6 1.4 collective-permute-start.3
  610.0 2.4 collective-permute-done.2
  612.4 4.5 collective-permute-done.3
  616.9 0.2 maximum_convert_fusion.1
  617.1 9.7 %fusion.104 = bf16[1,8,48,768]{3,2,1,0:T(8,128)(2,1)} fusion(f32[1,14,48,768]{3,2,1,0:T(8,128)S(1)} %maximum_convert_fusion.1, f32[768]{0:T(1024)S(1)} %get-tuple-element.114, f32[768]{0:T(1024)S(1)} %get-tuple-element.67, f32[768]{0:T(1024)S(1)} %get-tuple-element.68, f32[768]{0:T(1024)S(1)} %get-tuple-element.69, f32[768]{0:T(1024)S(1)} %get-tuple-element.70, ...), kind=kLoop, calls=%fused_computation.247 | loop fusion | flops 29491200 | bytes 11702272 | tf_op jit(solution)/shard_map/convert_element_type | solution.py:159
  626.8 23.9 %all-gather.15.cloned.1.call-done = f32[112,7,768]{2,1,0:T(8,128)} async-done(((f32[7,7,768]{2,1,0:T(8,128)}), f32[112,7,768]{2,1,0:T(8,128)}) %all-gather.15.cloned.1.call-update) | async-done | bytes 2408464 | tf_op jit(solution)/shard_map/all_gather | solution.py:160
  650.7 2.6 reduce_sum.545
  653.3 80.0 %all-gather.11.cloned.1.call-done = bf16[1536,3072]{1,0:T(8,128)(2,1)} async-done(((bf16[96,3072]{1,0:T(8,128)(2,1)}), bf16[1536,3072]{1,0:T(8,128)(2,1)}) %all-gather.11.cloned.1.call-update) | async-done | bytes 9437200 | tf_op jit(solution)/shard_map/all_gather | solution.py:42
  733.3 12.7 %convert_element_type.101 = f32[1536,3072]{1,0:T(8,128)} convert(bf16[1536,3072]{1,0:T(8,128)(2,1)} %all-gather.11.cloned.1.call-done) | non-fusion elementwise | flops 4718592 | bytes 28311552 | tf_op jit(solution)/shard_map/convert_element_type | solution.py:43
  746.0 69.0 %all-gather.13.cloned.1.call-done = bf16[3072,1536]{0,1:T(8,128)(2,1)} async-done(((bf16[3072,96]{0,1:T(8,128)(2,1)}), bf16[3072,1536]{0,1:T(8,128)(2,1)}) %all-gather.13.cloned.1.call-update) | async-done | bytes 9437200 | tf_op jit(solution)/shard_map/all_gather | solution.py:42
  814.9 13.5 %copy.17 = f32[3072,1536]{1,0:T(8,128)} copy(bf16[3072,1536]{0,1:T(8,128)(2,1)} %all-gather.13.cloned.1.call-done) | data formatting | bytes 28311552
  (96 shorter events, 0.8 us)
Async XLA Ops:
  7.2 13.2 %copy-start.2 = (bf16[1,8,48,768]{3,2,1,0:T(8,128)(2,1)S(1)}, bf16[1,8,48,768]{3,2,1,0:T(8,128)(2,1)}, u32[]{:S(2)}) copy-start(bf16[1,8,48,768]{3,2,1,0:T(8,128)(2,1)} %param.11) | copy-start | bytes 1769476
  7.2 61.6 %all-gather.7.cloned.1.call-start = ((), (), s32[]{:S(2)}) async-start(), calls=%async_computation.4 | async-start | bytes 1769472 | tf_op jit(solution)/shard_map/all_gather | solution.py:29
  8.4 10.1 %collective-permute-start = (bf16[1,3,48,768]{3,2,1,0:T(8,128)(2,1)S(1)}, bf16[1,3,48,768]{3,2,1,0:T(8,128)(2,1)S(1)}, u32[]{:S(2)}, u32[]{:S(2)}) collective-permute-start(bf16[1,3,48,768]{3,2,1,0:T(8,128)(2,1)S(1)} %get-tuple-element.121), channel_id=1, source_target_pairs={{0,2},{2,4},{4,6},{1,3},{3,5},{5,7},{8,10},{10,12},{12,14},{9,11},... | collective-permute-start | bytes 663560 | tf_op jit(solution)/shard_map/ppermute | solution.py:16
  12.4 7.9 collective-permute-start.1
  41.3 27.5 %copy-start.9 = (f32[3072]{0:T(1024)S(1)}, f32[3072]{0:T(1024)}, u32[]{:S(2)}) copy-start(f32[3072]{0:T(1024)} %param.17) | copy-start | bytes 36868
  42.4 87.5 %reduce-scatter.5.cloned.1.call-start = ((), (), s32[]{:S(2)}) async-start(), calls=%async_computation.5 | async-start | bytes 3538944 | tf_op jit(solution)/shard_map/reduce_scatter | solution.py:37
  85.7 1.4 copy-start.3
  94.9 35.0 %copy-start.7 = (f32[768]{0:T(1024)S(1)}, f32[768]{0:T(1024)}, u32[]{:S(2)}) copy-start(f32[768]{0:T(1024)} %param.20) | copy-start | bytes 9220
  94.9 35.0 %copy-start.8 = (f32[768]{0:T(1024)S(1)}, f32[768]{0:T(1024)}, u32[]{:S(2)}) copy-start(f32[768]{0:T(1024)} %param.19) | copy-start | bytes 9220
  94.9 60.7 %all-gather.9.cloned.1.call-start = ((), (), s32[]{:S(2)}) async-start(), calls=%async_computation.6 | async-start | bytes 1769472 | tf_op jit(solution)/shard_map/all_gather | solution.py:29
  132.8 75.4 %reduce-scatter.7.cloned.1.call-start = ((), (), s32[]{:S(2)}) async-start(), calls=%async_computation.7 | async-start | bytes 3538944 | tf_op jit(solution)/shard_map/reduce_scatter | solution.py:37
  164.0 1.4 copy-start.4
  173.2 233.6 %reduce-scatter.9.cloned.1.call-start = ((), (), s32[]{:S(2)}) async-start(), calls=%async_computation.8 | async-start | bytes 20054016 | tf_op jit(solution)/shard_map/reduce_scatter | solution.py:41
  184.4 420.1 %reduce-scatter.11.cloned.1.call-start = ((), (), s32[]{:S(2)}) async-start(), calls=%async_computation.10 | async-start | bytes 20054016 | tf_op jit(solution)/shard_map/reduce_scatter | solution.py:41
  195.9 454.8 %all-gather.15.cloned.1.call-start = ((), (), s32[]{:S(2)}) async-start(), calls=%async_computation.12 | async-start | bytes 2924544 | tf_op jit(solution)/shard_map/all_gather | solution.py:160
  215.5 5.1 copy-start
  224.4 0.7 copy-start.6
  225.1 508.2 %all-gather.11.cloned.1.call-start = ((), (), s32[]{:S(2)}) async-start(), calls=%async_computation.9 | async-start | bytes 10027008 | tf_op jit(solution)/shard_map/all_gather | solution.py:42
  409.0 197.7 %copy-start.1 = (bf16[384,768]{1,0:T(8,128)(2,1)S(1)}, bf16[384,768]{1,0:T(8,128)(2,1)}, u32[]{:S(2)}) copy-start(bf16[384,768]{1,0:T(8,128)(2,1)} %copy-done) | copy-start | bytes 1769476
  409.0 405.9 %all-gather.13.cloned.1.call-start = ((), (), s32[]{:S(2)}) async-start(), calls=%async_computation.11 | async-start | bytes 10027008 | tf_op jit(solution)/shard_map/all_gather | solution.py:42
  606.8 5.6 collective-permute-start.2
  608.6 8.5 %copy-start.5 = (bf16[1,8,48,768]{3,2,1,0:T(8,128)(2,1)S(1)}, bf16[1,8,48,768]{3,2,1,0:T(8,128)(2,1)}, u32[]{:S(2)}) copy-start(bf16[1,8,48,768]{3,2,1,0:T(8,128)(2,1)} %param.21) | copy-start | bytes 1769476
  608.6 8.3 collective-permute-start.3
Sparse Core Ops, SparseCore 0:
  42.5 26.2 all-gather.6
  95.0 34.7 reduce-scatter.4
  132.9 22.7 all-gather.8
  173.3 34.7 reduce-scatter.6
  212.7 194.1 reduce-scatter.8
  411.4 193.1 reduce-scatter.10
  607.4 43.1 all-gather.14
  653.5 79.6 all-gather.10
  735.6 79.3 all-gather.12
